TPU v7x, 32 devices: a whole 2x2x4 slice. The times are simulated.
32 devices in a mesh: row: 16 (over z, x, core), col: 2 (over y).
Axes of the slice: x: 2, y: 2, z: 4, core: 2. Of those that a mesh axis runs over, the one named last changes fastest.
Arguments:
- row_features: bfloat16 [256, 256], P(('row', 'col')), may hold values from -6 to 6
- col_features: bfloat16 [512, 256], P(('col', 'row')), may hold values from -6 to 6
- row_proj: bfloat16 [256, 64], replicated, may hold values from -0.375 to 0.375
- col_proj: bfloat16 [256, 64], replicated, may hold values from -0.375 to 0.375
- pair_weight: bfloat16 [2, 3, 3, 64, 64], replicated, may hold values from -0.1875 to 0.1875
- pair_bias: float32 [64], replicated, may hold values from -4 to 4
- conv_weight: bfloat16 [3, 3, 64, 64], replicated, may hold values from -0.25 to 0.25
- dilations: int32 [2], replicated, may hold values from 1 to 8, as said below
- cotangent: bfloat16 [64, 256, 512], P(None, 'row', 'col'), may hold values from -6 to 6
Outputs:
- pair_out: bfloat16 [64, 256, 512], P(None, 'row', 'col')
- grad_row_features: float32 [256, 256], P(('row', 'col'))
- grad_col_features: float32 [512, 256], P(('col', 'row'))
- grad_row_proj: float32 [256, 64], replicated
- grad_col_proj: float32 [256, 64], replicated
- grad_pair_weight: float32 [2, 3, 3, 64, 64], replicated
- grad_pair_bias: float32 [64], replicated
- grad_conv_weight: float32 [3, 3, 64, 64], replicated
Inputs may be any that keep to these rules, and one draw needn't show every extreme that they name: One of the two dilations equals 8.
All inputs are finite; a program needn't handle non-finite values.
Results may differ from a plain program's by a relative error of at most 0.0054.
Values may be sent and summed in bfloat16 or wider, within the bound.
No kernel may reach another device: no remote copies, remote signals or barrier semaphores. Data moves between devices by JAX's collectives and lax.ppermute only.
A program may use at most 64 MiB of HBM per device.

v0:
```python
import jax
import jax.numpy as jnp
from jax import lax
from jax.sharding import PartitionSpec as P

MAX_DILATION = 8


def padded_2(value, sides, width):
    for axis, dim in sides:
        devices, length = (lax.axis_size(axis), value.shape[dim])
        up = [(i, (i + 1) % devices) for i in range(devices - 1)]
        down = [(j, i) for i, j in up]
        last = lax.slice_in_dim(value, length - width, length, axis=dim)
        leading = lax.slice_in_dim(value, 0, width, axis=dim)
        before = lax.ppermute(last, axis, up)
        after = lax.ppermute(leading, axis, down)
        value = jnp.concatenate([before, value, after], axis=dim)
    return value


def project(features, weight):
    return jnp.dot(features, weight, preferred_element_type=jnp.float32).astype(jnp.bfloat16)


def line_terms(padded, weights, dilation, count, offset):
    shifted = jnp.stack(
        [
            lax.dynamic_slice_in_dim(padded, offset + (tap_idx - 1) * dilation, count, 0)
            for tap_idx in range(3)
        ]
    )
    return jnp.einsum("kip,kqpo->qio", shifted, weights, preferred_element_type=jnp.float32)


def line_valid(first_cell, count, cell_limit, dilation):
    cells = first_cell + jnp.arange(count, dtype=jnp.int32)
    columns = [
        (cells + (tap_idx - 1) * dilation >= 0) & (cells + (tap_idx - 1) * dilation < cell_limit)
        for tap_idx in range(3)
    ]
    return jnp.stack(columns, axis=1).astype(jnp.float32)


def pair_field(row_terms, col_terms, row_valid, col_valid, bias):
    from_rows = jnp.einsum("jq,qic->cij", col_valid, row_terms, precision=lax.Precision.HIGHEST)
    from_cols = jnp.einsum("ik,kjc->cij", row_valid, col_terms, precision=lax.Precision.HIGHEST)
    return from_rows + from_cols + bias[:, None, None]


def window_at(padded, row_index, col_index, rows, cols):
    anchor = jnp.zeros((), jnp.int32)
    return lax.dynamic_slice(padded, (anchor, row_index, col_index), (padded.shape[0], rows, cols))


def conv_taps(padded, weight, dilation, rows, cols, margin):
    result = jnp.zeros((weight.shape[3], rows, cols), jnp.float32)
    for tap_row in range(3):
        for tap_col in range(3):
            window = window_at(
                padded,
                margin + (tap_row - 1) * dilation,
                margin + (tap_col - 1) * dilation,
                rows,
                cols,
            )
            result = result + jnp.einsum(
                "co,cij->oij", weight[tap_row, tap_col], window, preferred_element_type=jnp.float32
            )
    return result


def back_taps(padded, weight, dilation, rows, cols, margin):
    result = jnp.zeros((weight.shape[2], rows, cols), jnp.float32)
    for tap_row in range(3):
        for tap_col in range(3):
            window = window_at(
                padded,
                margin - (tap_row - 1) * dilation,
                margin - (tap_col - 1) * dilation,
                rows,
                cols,
            )
            result = result + jnp.einsum(
                "co,oij->cij", weight[tap_row, tap_col], window, preferred_element_type=jnp.float32
            )
    return result


def tap_grads(hidden_pad, grads, dilation, rows, cols, margin):
    stacked = []
    for tap_row in range(3):
        line_list = []
        for tap_col in range(3):
            window = window_at(
                hidden_pad,
                margin + (tap_row - 1) * dilation,
                margin + (tap_col - 1) * dilation,
                rows,
                cols,
            )
            line_list.append(
                jnp.einsum("cij,oij->co", window, grads, preferred_element_type=jnp.float32)
            )
        stacked.append(jnp.stack(line_list))
    return jnp.stack(stacked)


def shards(
    row_features,
    col_features,
    row_proj,
    col_proj,
    pair_weight,
    pair_bias,
    conv_weight,
    dilations,
    cotangent,
):
    first_rate = dilations[0]
    second_rate = dilations[1]
    margin = MAX_DILATION
    row_count = lax.axis_size("row")
    col_count = lax.axis_size("col")
    row_place = lax.axis_index("row")
    col_place = lax.axis_index("col")
    rows_here = cotangent.shape[1]
    cols_here = cotangent.shape[2]
    row_start = row_place * rows_here
    col_start = col_place * cols_here
    row_limit = rows_here * row_count
    col_limit = cols_here * col_count
    row_piece = row_features.shape[0]
    col_piece = col_features.shape[0]
    rows_a = lax.all_gather(project(row_features, row_proj), "col", axis=0, tiled=True)
    cols_b = lax.all_gather(project(col_features, col_proj), "row", axis=0, tiled=True)
    pad_extra = 0
    a_pad = padded_2(rows_a, (("row", 0),), MAX_DILATION)
    b_pad = padded_2(cols_b, (("col", 0),), MAX_DILATION)
    row_terms = line_terms(
        a_pad, pair_weight[0], first_rate, rows_here + 2 * pad_extra, margin - pad_extra
    )
    col_terms = line_terms(
        b_pad,
        jnp.swapaxes(pair_weight[1], 0, 1),
        first_rate,
        cols_here + 2 * pad_extra,
        margin - pad_extra,
    )
    row_valid = line_valid(row_start - pad_extra, rows_here + 2 * pad_extra, row_limit, first_rate)
    col_valid = line_valid(col_start - pad_extra, cols_here + 2 * pad_extra, col_limit, first_rate)
    pre_act = pair_field(row_terms, col_terms, row_valid, col_valid, pair_bias)
    hidden_own = jax.nn.silu(pre_act).astype(jnp.bfloat16)
    hidden = padded_2(hidden_own, (("row", 1), ("col", 2)), MAX_DILATION)
    conv_mixed = conv_taps(hidden, conv_weight, second_rate, rows_here, cols_here, margin)
    pair_out = (hidden_own.astype(jnp.float32) + conv_mixed).astype(jnp.bfloat16)
    grad_pad = padded_2(cotangent, (("row", 1), ("col", 2)), MAX_DILATION)
    d_hidden = cotangent.astype(jnp.float32) + back_taps(
        grad_pad, conv_weight, second_rate, rows_here, cols_here, margin
    )
    conv_grad = tap_grads(hidden, cotangent, second_rate, rows_here, cols_here, margin)
    sigmoid_own = jax.nn.sigmoid(pre_act)
    d_pre = d_hidden * sigmoid_own * (1.0 + pre_act * (1.0 - sigmoid_own))
    bias_grad = jnp.sum(d_pre, axis=(1, 2))
    row_valid_own = line_valid(row_start, rows_here, row_limit, first_rate)
    col_valid_own = line_valid(col_start, cols_here, col_limit, first_rate)
    row_part = jnp.einsum("jq,cij->qic", col_valid_own, d_pre, precision=lax.Precision.HIGHEST)
    col_part = jnp.einsum("ik,cij->kjc", row_valid_own, d_pre, precision=lax.Precision.HIGHEST)
    row_sums = lax.psum(row_part, "col")
    col_sums = lax.psum(col_part, "row")
    back_rows = jnp.einsum(
        "qio,kqpo->kip",
        row_sums,
        pair_weight[0].astype(jnp.float32),
        precision=lax.Precision.HIGHEST,
    )
    back_cols = jnp.einsum(
        "kjo,kqpo->qjp",
        col_sums,
        pair_weight[1].astype(jnp.float32),
        precision=lax.Precision.HIGHEST,
    )
    rows_back_pad = padded_2(back_rows, (("row", 1),), MAX_DILATION)
    cols_back_pad = padded_2(back_cols, (("col", 1),), MAX_DILATION)
    row_own = col_place * row_piece
    col_own = row_place * col_piece
    d_rows = sum(
        (
            lax.dynamic_slice_in_dim(
                rows_back_pad[tap_idx], margin + row_own - (tap_idx - 1) * first_rate, row_piece, 0
            )
            for tap_idx in range(3)
        )
    )
    d_cols = sum(
        (
            lax.dynamic_slice_in_dim(
                cols_back_pad[tap_idx], margin + col_own - (tap_idx - 1) * first_rate, col_piece, 0
            )
            for tap_idx in range(3)
        )
    )
    d_rows = d_rows.astype(jnp.bfloat16)
    d_cols = d_cols.astype(jnp.bfloat16)
    grad_row_features = jnp.dot(d_rows, row_proj.T, preferred_element_type=jnp.float32)
    grad_col_features = jnp.dot(d_cols, col_proj.T, preferred_element_type=jnp.float32)
    grad_row_proj = jnp.dot(row_features.T, d_rows, preferred_element_type=jnp.float32)
    grad_col_proj = jnp.dot(col_features.T, d_cols, preferred_element_type=jnp.float32)
    row_shifted = jnp.stack(
        [
            lax.dynamic_slice_in_dim(
                a_pad, margin + row_own + (tap_idx - 1) * first_rate, row_piece, 0
            )
            for tap_idx in range(3)
        ]
    )
    col_shifted = jnp.stack(
        [
            lax.dynamic_slice_in_dim(
                b_pad, margin + col_own + (tap_idx - 1) * first_rate, col_piece, 0
            )
            for tap_idx in range(3)
        ]
    )
    row_sums_own = lax.dynamic_slice_in_dim(row_sums, row_own, row_piece, 1)
    col_sums_own = lax.dynamic_slice_in_dim(col_sums, col_own, col_piece, 1)
    grad_row_pair = jnp.einsum(
        "kip,qio->kqpo",
        row_shifted.astype(jnp.float32),
        row_sums_own,
        precision=lax.Precision.HIGHEST,
    )
    grad_col_pair = jnp.einsum(
        "qjp,kjo->kqpo",
        col_shifted.astype(jnp.float32),
        col_sums_own,
        precision=lax.Precision.HIGHEST,
    )
    summed = lax.psum(
        (
            grad_row_proj,
            grad_col_proj,
            jnp.stack([grad_row_pair, grad_col_pair]),
            bias_grad,
            conv_grad,
        ),
        ("row", "col"),
    )
    return (
        pair_out,
        grad_row_features,
        grad_col_features,
        summed[0],
        summed[1],
        summed[2],
        summed[3],
        summed[4],
    )


def solution(mesh):
    return jax.shard_map(
        shards,
        mesh=mesh,
        in_specs=(
            P(("row", "col"), None),
            P(("col", "row"), None),
            P(),
            P(),
            P(),
            P(),
            P(),
            P(),
            P(None, "row", "col"),
        ),
        out_specs=(
            P(None, "row", "col"),
            P(("row", "col"), None),
            P(("col", "row"), None),
            P(),
            P(),
            P(),
            P(),
            P(),
        ),
        check_vma=False,
    )
```

profile of v0, /device:TPU:0, one launch (start us, length us, event | category | flops | bytes accessed | tf_op | source)
XLA Modules:
  0.0 352.3 jit_solution(3747171923452874970)
XLA Ops:
  8.7 23.3 %all_gather.7 = bf16[256,64]{1,0:T(8,128)(2,1)S(1)} all-gather(bf16[16,64]{1,0:T(8,128)(2,1)S(1)} %convolution_convert_fusion), channel_id=1, replica_groups=mesh['row'=16,'col'=2] {'row'}, dimensions={0}, use_global_device_ids=true | all-gather | bytes 34816 | tf_op jit(solution)/shard_map/all_gather | solution.py:136
  32.0 3.4 collective-permute-start.2
  35.4 1.3 collective-permute-start.3
  37.6 5.0 %all_gather.6 = bf16[16,64]{1,0:T(8,128)(2,1)S(1)} all-gather(bf16[8,64]{1,0:T(8,128)(2,1)S(1)} %convolution_convert_fusion.1), channel_id=1, replica_groups=mesh['row'=16,'col'=2] {'col'}, dimensions={0}, use_global_device_ids=true | all-gather | bytes 3072 | tf_op jit(solution)/shard_map/all_gather | solution.py:135
  42.6 1.3 collective-permute-start
  43.9 1.3 collective-permute-start.1
  47.0 3.7 %collective-permute-start.8 = (bf16[64,8,256]{2,0,1:T(8,128)(2,1)}, bf16[64,8,256]{2,0,1:T(8,128)(2,1)}, u32[]{:S(2)}, u32[]{:S(2)}) collective-permute-start(bf16[64,8,256]{2,0,1:T(8,128)(2,1)} %copy.143), channel_id=1, source_target_pairs={{0,2},{2,4},{4,6},{6,8},{8,10},{10,12},{12,14},{14,16},{16,18},{18... | collective-permute-start | bytes 786440 | tf_op jit(solution)/shard_map/ppermute | solution.py:16
  64.3 1.3 collective-permute-start.9
  67.0 1.4 multiply_convert_fusion
  68.8 3.0 collective-permute-start.4
  71.8 1.3 collective-permute-start.5
  75.0 4.0 %collective-permute-start.10 = (bf16[64,32,8]{2,0,1:T(8,128)(2,1)S(1)}, bf16[64,32,8]{2,0,1:T(8,128)(2,1)S(1)}, u32[]{:S(2)}, u32[]{:S(2)}) collective-permute-start(bf16[64,32,8]{2,0,1:T(8,128)(2,1)S(1)} %get-tuple-element.20), channel_id=1, source_target_pairs={{0,1},{2,3},{4,5},{6,7},{8,9},{10,11},{12,13},{14,15},{16,17},{18,... | collective-permute-start | bytes 98312 | tf_op jit(solution)/shard_map/ppermute | solution.py:16
  79.0 1.3 collective-permute-start.11
  81.7 5.4 %collective-permute-start.6 = (bf16[64,32,8]{2,0,1:T(8,128)(2,1)}, bf16[64,32,8]{2,0,1:T(8,128)(2,1)}, u32[]{:S(2)}, u32[]{:S(2)}) collective-permute-start(bf16[64,32,8]{2,0,1:T(8,128)(2,1)} %get-tuple-element.22), channel_id=1, source_target_pairs={{0,1},{2,3},{4,5},{6,7},{8,9},{10,11},{12,13},{14,15},{16,17},{18,... | collective-permute-start | bytes 98312 | tf_op jit(solution)/shard_map/ppermute | solution.py:16
  87.1 1.5 collective-permute-start.7
  88.6 2.0 collective-permute-done.10
  90.5 4.7 %collective-permute-done.11 = bf16[64,32,8]{2,0,1:T(8,128)(2,1)S(1)} collective-permute-done((bf16[64,32,8]{2,0,1:T(8,128)(2,1)S(1)}, bf16[64,32,8]{2,0,1:T(8,128)(2,1)S(1)}, u32[]{:S(2)}, u32[]{:S(2)}) %collective-permute-start.11) | collective-permute-done | bytes 32800 | tf_op jit(solution)/shard_map/ppermute | solution.py:17
  100.2 1.8 convolution_bitcast_fusion.7
  103.0 8.6 %psum.49 = f32[3,16,64]{1,0,2:T(4,128)S(1)} all-reduce(f32[3,16,64]{1,0,2:T(4,128)S(1)} %bitcast.308), channel_id=1, replica_groups=mesh['row'=16,'col'=2] {'col'}, use_global_device_ids=true, to_apply=%region_0.1 | all-reduce | flops 3072 | bytes 24576 | tf_op jit(solution)/shard_map/psum | solution.py:169
  113.1 1.5 collective-permute-start.12
  114.6 1.3 collective-permute-start.13
  116.2 47.7 %psum.54 = f32[64]{0:T(128)} all-reduce(f32[64]{0:T(128)S(1)} %get-tuple-element.56), channel_id=1, replica_groups=mesh['row'=16,'col'=2] {'row','col'}, use_global_device_ids=true, to_apply=%region_6.7 | all-reduce | flops 64 | bytes 512 | tf_op jit(solution)/shard_map/psum | solution.py:239
  163.9 2.2 pad_maximum_fusion
  176.3 19.0 %all-reduce.4.cloned.1.call-done = f32[3,256,64]{1,0,2:T(4,128)} async-done(((f32[3,256,64]{1,0,2:T(4,128)}), f32[3,256,64]{1,0,2:T(4,128)}) %all-reduce.4.cloned.1.call-update) | async-done | bytes 196624 | tf_op jit(solution)/shard_map/psum | solution.py:170
  196.4 1.3 convolution_bitcast_fusion.8
  197.8 3.5 collective-permute-start.14
  201.3 1.3 collective-permute-start.15
  203.8 4.1 %collective-permute-done.15 = f32[3,8,64]{1,2,0:T(8,128)S(1)} collective-permute-done((f32[3,8,64]{1,2,0:T(8,128)S(1)}, f32[3,8,64]{1,2,0:T(8,128)S(1)}, u32[]{:S(2)}, u32[]{:S(2)}) %collective-permute-start.15) | collective-permute-done | bytes 6176 | tf_op jit(solution)/shard_map/ppermute | solution.py:17
  210.5 129.1 %all-reduce.6.cloned.1.call-done = (f32[256,64]{0,1:T(8,128)}, f32[256,64]{0,1:T(8,128)}, f32[2,3,3,64,64]{3,4,1,2,0:T(8,128)}, f32[3,3,64,64]{3,2,1,0:T(8,128)}) async-done(((f32[256,64]{0,1:T(8,128)}, f32[256,64]{0,1:T(8,128)}, f32[2,3,3,64,64]{3,4,1,2,0:T(8,128)}, f32[3,3,64,64]{3,2,1,0:T(8,128)}), (f32[256,64]{0,1:T(8,128)}, f32[256,64]{0,1:T(8,128)}, f32[2,3,3,64,64]{3,4,1,2,0:T(8,128)}, ...) | async-done | bytes 573456 | tf_op jit(solution)/shard_map/psum | solution.py:239
  339.6 2.1 copy.59
  341.8 1.5 copy.158
  343.2 1.5 copy.159
  (133 shorter events, 35.9 us)
Async XLA Ops:
  7.2 0.8 copy-start
  7.2 56.0 %copy-start.1 = (bf16[64,16,256]{2,1,0:T(8,128)(2,1)S(1)}, bf16[64,16,256]{2,1,0:T(8,128)(2,1)}, u32[]{:S(2)}) copy-start(bf16[64,16,256]{2,1,0:T(8,128)(2,1)} %param.17) | copy-start | bytes 1572868
  7.2 43.5 %copy-start.12 = (s32[2]{0:T(128)S(1)}, s32[2]{0:T(128)}, u32[]{:S(2)}) copy-start(s32[2]{0:T(128)} %param.16) | copy-start | bytes 28
  7.2 188.1 %all-reduce.4.cloned.1.call-start = ((), (), s32[]{:S(2)}) async-start(), calls=%async_computation | async-start | bytes 524288 | tf_op jit(solution)/shard_map/psum | solution.py:170
  32.0 32.3 %collective-permute-start.2 = (bf16[8,64]{1,0:T(8,128)(2,1)S(1)}, bf16[8,64]{1,0:T(8,128)(2,1)S(1)}, u32[]{:S(2)}, u32[]{:S(2)}) collective-permute-start(bf16[8,64]{1,0:T(8,128)(2,1)S(1)} %get-tuple-element.39), channel_id=1, source_target_pairs={{0,1},{2,3},{4,5},{6,7},{8,9},{10,11},{12,13},{14,15},{16,17},{18,... | collective-permute-start | bytes 3080 | tf_op jit(solution)/shard_map/ppermute | solution.py:16
  35.4 30.3 %collective-permute-start.3 = (bf16[8,64]{1,0:T(8,128)(2,1)S(1)}, bf16[8,64]{1,0:T(8,128)(2,1)S(1)}, u32[]{:S(2)}, u32[]{:S(2)}) collective-permute-start(bf16[8,64]{1,0:T(8,128)(2,1)S(1)} %get-tuple-element.38), channel_id=1, source_target_pairs={{1,0},{3,2},{5,4},{7,6},{9,8},{11,10},{13,12},{15,14},{17,16},{19,... | collective-permute-start | bytes 3080 | tf_op jit(solution)/shard_map/ppermute | solution.py:17
  42.6 23.2 %collective-permute-start = (bf16[8,64]{1,0:T(8,128)(2,1)S(1)}, bf16[8,64]{1,0:T(8,128)(2,1)S(1)}, u32[]{:S(2)}, u32[]{:S(2)}) collective-permute-start(bf16[8,64]{1,0:T(8,128)(2,1)S(1)} %get-tuple-element.51), channel_id=1, source_target_pairs={{0,2},{2,4},{4,6},{6,8},{8,10},{10,12},{12,14},{14,16},{16,18},{18... | collective-permute-start | bytes 3080 | tf_op jit(solution)/shard_map/ppermute | solution.py:16
  43.9 21.9 %collective-permute-start.1 = (bf16[8,64]{1,0:T(8,128)(2,1)S(1)}, bf16[8,64]{1,0:T(8,128)(2,1)S(1)}, u32[]{:S(2)}, u32[]{:S(2)}) collective-permute-start(bf16[8,64]{1,0:T(8,128)(2,1)S(1)} %get-tuple-element.50), channel_id=1, source_target_pairs={{2,0},{4,2},{6,4},{8,6},{10,8},{12,10},{14,12},{16,14},{18,16},{20... | collective-permute-start | bytes 3080 | tf_op jit(solution)/shard_map/ppermute | solution.py:17
  46.2 19.6 %copy-start.7 = (bf16[2,3,3,64,64]{4,3,2,1,0:T(8,128)(2,1)S(1)}, bf16[2,3,3,64,64]{4,3,2,1,0:T(8,128)(2,1)}, u32[]{:S(2)}) copy-start(bf16[2,3,3,64,64]{4,3,2,1,0:T(8,128)(2,1)} %param.13) | copy-start | bytes 442372
  47.0 26.5 %collective-permute-start.8 = (bf16[64,8,256]{2,0,1:T(8,128)(2,1)}, bf16[64,8,256]{2,0,1:T(8,128)(2,1)}, u32[]{:S(2)}, u32[]{:S(2)}) collective-permute-start(bf16[64,8,256]{2,0,1:T(8,128)(2,1)} %copy.143), channel_id=1, source_target_pairs={{0,2},{2,4},{4,6},{6,8},{8,10},{10,12},{12,14},{14,16},{16,18},{18... | collective-permute-start | bytes 786440 | tf_op jit(solution)/shard_map/ppermute | solution.py:16
  64.3 2.7 copy-start.13
  64.3 10.3 %collective-permute-start.9 = (bf16[64,8,256]{2,0,1:T(8,128)(2,1)}, bf16[64,8,256]{2,0,1:T(8,128)(2,1)S(1)}, u32[]{:S(2)}, u32[]{:S(2)}) collective-permute-start(bf16[64,8,256]{2,0,1:T(8,128)(2,1)} %copy.144), channel_id=1, source_target_pairs={{2,0},{4,2},{6,4},{8,6},{10,8},{12,10},{14,12},{16,14},{18,16},{20... | collective-permute-start | bytes 786440 | tf_op jit(solution)/shard_map/ppermute | solution.py:17
  68.4 4.8 %copy-start.4 = (bf16[3,3,64,64]{3,2,1,0:T(8,128)(2,1)S(1)}, bf16[3,3,64,64]{3,2,1,0:T(8,128)(2,1)}, u32[]{:S(2)}) copy-start(bf16[3,3,64,64]{3,2,1,0:T(8,128)(2,1)} %param.15) | copy-start | bytes 221188
  68.8 11.5 %collective-permute-start.4 = (bf16[64,8,256]{2,0,1:T(8,128)(2,1)S(1)}, bf16[64,8,256]{2,0,1:T(8,128)(2,1)S(1)}, u32[]{:S(2)}, u32[]{:S(2)}) collective-permute-start(bf16[64,8,256]{2,0,1:T(8,128)(2,1)S(1)} %get-tuple-element.26), channel_id=1, source_target_pairs={{0,2},{2,4},{4,6},{6,8},{8,10},{10,12},{12,14},{14,16},{16,18},{18... | collective-permute-start | bytes 786440 | tf_op jit(solution)/shard_map/ppermute | solution.py:16
  71.8 8.5 %collective-permute-start.5 = (bf16[64,8,256]{2,0,1:T(8,128)(2,1)S(1)}, bf16[64,8,256]{2,0,1:T(8,128)(2,1)S(1)}, u32[]{:S(2)}, u32[]{:S(2)}) collective-permute-start(bf16[64,8,256]{2,0,1:T(8,128)(2,1)S(1)} %get-tuple-element.27), channel_id=1, source_target_pairs={{2,0},{4,2},{6,4},{8,6},{10,8},{12,10},{14,12},{16,14},{18,16},{20... | collective-permute-start | bytes 786440 | tf_op jit(solution)/shard_map/ppermute | solution.py:17
  75.0 15.6 %collective-permute-start.10 = (bf16[64,32,8]{2,0,1:T(8,128)(2,1)S(1)}, bf16[64,32,8]{2,0,1:T(8,128)(2,1)S(1)}, u32[]{:S(2)}, u32[]{:S(2)}) collective-permute-start(bf16[64,32,8]{2,0,1:T(8,128)(2,1)S(1)} %get-tuple-element.20), channel_id=1, source_target_pairs={{0,1},{2,3},{4,5},{6,7},{8,9},{10,11},{12,13},{14,15},{16,17},{18,... | collective-permute-start | bytes 98312 | tf_op jit(solution)/shard_map/ppermute | solution.py:16
  79.0 16.3 %collective-permute-start.11 = (bf16[64,32,8]{2,0,1:T(8,128)(2,1)S(1)}, bf16[64,32,8]{2,0,1:T(8,128)(2,1)S(1)}, u32[]{:S(2)}, u32[]{:S(2)}) collective-permute-start(bf16[64,32,8]{2,0,1:T(8,128)(2,1)S(1)} %get-tuple-element.21), channel_id=1, source_target_pairs={{1,0},{3,2},{5,4},{7,6},{9,8},{11,10},{13,12},{15,14},{17,16},{19,... | collective-permute-start | bytes 98312 | tf_op jit(solution)/shard_map/ppermute | solution.py:17
  80.3 1.4 copy-start.2
  81.7 82.2 %collective-permute-start.6 = (bf16[64,32,8]{2,0,1:T(8,128)(2,1)}, bf16[64,32,8]{2,0,1:T(8,128)(2,1)}, u32[]{:S(2)}, u32[]{:S(2)}) collective-permute-start(bf16[64,32,8]{2,0,1:T(8,128)(2,1)} %get-tuple-element.22), channel_id=1, source_target_pairs={{0,1},{2,3},{4,5},{6,7},{8,9},{10,11},{12,13},{14,15},{16,17},{18,... | collective-permute-start | bytes 98312 | tf_op jit(solution)/shard_map/ppermute | solution.py:16
  87.1 76.8 %collective-permute-start.7 = (bf16[64,32,8]{2,0,1:T(8,128)(2,1)}, bf16[64,32,8]{2,0,1:T(8,128)(2,1)}, u32[]{:S(2)}, u32[]{:S(2)}) collective-permute-start(bf16[64,32,8]{2,0,1:T(8,128)(2,1)} %get-tuple-element.23), channel_id=1, source_target_pairs={{1,0},{3,2},{5,4},{7,6},{9,8},{11,10},{13,12},{15,14},{17,16},{19,... | collective-permute-start | bytes 98312 | tf_op jit(solution)/shard_map/ppermute | solution.py:17
  102.8 61.1 %copy-start.3 = (bf16[64,8,256]{2,0,1:T(8,128)(2,1)S(1)}, bf16[64,8,256]{2,0,1:T(8,128)(2,1)}, u32[]{:S(2)}) copy-start(bf16[64,8,256]{2,0,1:T(8,128)(2,1)} %copy-done.2) | copy-start | bytes 786436
  102.8 236.8 %all-reduce.6.cloned.1.call-start = ((), (), s32[]{:S(2)}) async-start(), calls=%async_computation.1 | async-start | bytes 2031616 | tf_op jit(solution)/shard_map/psum | solution.py:239
  113.1 62.3 %collective-permute-start.12 = (f32[3,8,64]{2,1,0:T(8,128)S(1)}, f32[3,8,64]{2,1,0:T(8,128)S(1)}, u32[]{:S(2)}, u32[]{:S(2)}) collective-permute-start(f32[3,8,64]{2,1,0:T(8,128)S(1)} %get-tuple-element.43), channel_id=1, source_target_pairs={{0,2},{2,4},{4,6},{6,8},{8,10},{10,12},{12,14},{14,16},{16,18},{18... | collective-permute-start | bytes 18440 | tf_op jit(solution)/shard_map/ppermute | solution.py:16
  114.6 60.8 %collective-permute-start.13 = (f32[3,8,64]{2,1,0:T(8,128)S(1)}, f32[3,8,64]{2,1,0:T(8,128)S(1)}, u32[]{:S(2)}, u32[]{:S(2)}) collective-permute-start(f32[3,8,64]{2,1,0:T(8,128)S(1)} %get-tuple-element.44), channel_id=1, source_target_pairs={{2,0},{4,2},{6,4},{8,6},{10,8},{12,10},{14,12},{16,14},{18,16},{20... | collective-permute-start | bytes 18440 | tf_op jit(solution)/shard_map/ppermute | solution.py:17
  168.6 1.4 copy-start.5
  173.5 1.9 copy-start.11
  173.5 22.9 %copy-start.8 = (bf16[2,3,3,64,64]{4,3,2,1,0:T(8,128)(2,1)S(1)}, bf16[2,3,3,64,64]{4,3,2,1,0:T(8,128)(2,1)}, u32[]{:S(2)}) copy-start(bf16[2,3,3,64,64]{4,3,2,1,0:T(8,128)(2,1)} %param.13) | copy-start | bytes 442372
  197.7 10.6 %copy-start.10 = (bf16[16,256]{1,0:T(8,128)(2,1)S(1)}, bf16[16,256]{1,0:T(8,128)(2,1)}, u32[]{:S(2)}) copy-start(bf16[16,256]{1,0:T(8,128)(2,1)} %param.10) | copy-start | bytes 24580
  197.8 6.0 %collective-permute-start.14 = (f32[3,8,64]{1,2,0:T(8,128)S(1)}, f32[3,8,64]{1,2,0:T(8,128)S(1)}, u32[]{:S(2)}, u32[]{:S(2)}) collective-permute-start(f32[3,8,64]{1,2,0:T(8,128)S(1)} %get-tuple-element.31), channel_id=1, source_target_pairs={{0,1},{2,3},{4,5},{6,7},{8,9},{10,11},{12,13},{14,15},{16,17},{18,... | collective-permute-start | bytes 18440 | tf_op jit(solution)/shard_map/ppermute | solution.py:16
  201.3 6.6 %collective-permute-start.15 = (f32[3,8,64]{1,2,0:T(8,128)S(1)}, f32[3,8,64]{1,2,0:T(8,128)S(1)}, u32[]{:S(2)}, u32[]{:S(2)}) collective-permute-start(f32[3,8,64]{1,2,0:T(8,128)S(1)} %get-tuple-element.32), channel_id=1, source_target_pairs={{1,0},{3,2},{5,4},{7,6},{9,8},{11,10},{13,12},{15,14},{17,16},{19,... | collective-permute-start | bytes 18440 | tf_op jit(solution)/shard_map/ppermute | solution.py:17
  202.9 6.1 %copy-start.9 = (bf16[256,64]{0,1:T(8,128)(2,1)S(1)}, bf16[256,64]{0,1:T(8,128)(2,1)}, u32[]{:S(2)}) copy-start(bf16[256,64]{0,1:T(8,128)(2,1)} %param.11) | copy-start | bytes 98308
  339.6 5.1 %copy-start.6 = (f32[3,3,64,64]{3,2,1,0:T(8,128)S(1)}, f32[3,3,64,64]{3,2,1,0:T(8,128)}, u32[]{:S(2)}) copy-start(f32[3,3,64,64]{3,2,1,0:T(8,128)} %get-tuple-element.69) | copy-start | bytes 442372
Sparse Core Ops, SparseCore 0:
  102.9 92.3 all-reduce.3
  209.1 130.4 all-reduce.5
where the time goes:
time: 353 us; the launch traced here: 352 us
  waiting for transfers between devices  159 us (45%)
  blocking collectives  84.6 us (24%)
  starting transfers between devices  36.4 us (10%)
  matrix products  25.6 us (7%)
  between operations  24.7 us (7%)
  local copies, waits for them, and re-layouts  15.2 us (4%)
  other arithmetic  6.69 us (2%)
    psum x1, waiting for transfers between devices, shards(): lax.psum((grad_row_proj, grad_col_proj, jnp.stack([grad_row_pair, grad_co...  129 us
    psum x1, blocking collectives, shards(): lax.psum((grad_row_proj, grad_col_proj, jnp.stack([grad_row_pair, grad_co...  47.7 us
    ppermute x8, starting transfers between devices, padded_2(): before = lax.ppermute(last, axis, up)  25.9 us
    all_gather x1, blocking collectives, shards(): lax.all_gather(project(col_features, col_proj), 'row', axis=0, tiled=True)  23.3 us
    psum x1, waiting for transfers between devices, shards(): col_sums = lax.psum(col_part, 'row')  19 us
    ppermute x8, starting transfers between devices, padded_2(): after = lax.ppermute(leading, axis, down)  10.5 us
    unnamed x41, local copies, waits for them, and re-layouts  10.3 us
    ppermute x8, waiting for transfers between devices, padded_2(): after = lax.ppermute(leading, axis, down)  8.83 us
  transfers between devices with their start and end apart: 18, of which 5 were waited for; matrix products, arithmetic and copies ran while one was open for 10% of the time, Pallas kernels for 0%

commit v1 on v0

--- a/solution.py
+++ b/solution.py
@@ -133,7 +133,12 @@
     row_piece = row_features.shape[0]
     col_piece = col_features.shape[0]
     rows_a = lax.all_gather(project(row_features, row_proj), "col", axis=0, tiled=True)
-    cols_b = lax.all_gather(project(col_features, col_proj), "row", axis=0, tiled=True)
+    cols_b = jnp.concatenate(
+        lax.all_to_all(
+            jnp.stack([project(col_features, col_proj)] * lax.axis_size("row")), "row", 0, 0
+        ),
+        axis=0,
+    )
     pad_extra = 0
     a_pad = padded_2(rows_a, (("row", 0),), MAX_DILATION)
     b_pad = padded_2(cols_b, (("col", 0),), MAX_DILATION)

time: 353 us -> 346 us (0.980)
  blocking collectives: 84.6 us -> 60.9 us
  starting transfers between devices: 36.4 us -> 42.4 us
  matrix products: 25.6 us -> 30.2 us
  local copies, waits for them, and re-layouts: 15.2 us -> 18.8 us
    all_gather x1 -> x0, blocking collectives: 23.3 us -> none  [shards(): lax.all_gather(project(col_features, col_proj), 'row', axis=0, tiled=True)]
    psum x1, waiting for transfers between devices: 19 us -> 2.23 us  [shards(): col_sums = lax.psum(col_part, 'row')]
    ppermute x8, waiting for transfers between devices: 2 us -> 16.7 us  [padded_2(): before = lax.ppermute(last, axis, up)]
    ppermute x8, waiting for transfers between devices: 8.83 us -> 17.1 us  [padded_2(): after = lax.ppermute(leading, axis, down)]
    all_to_all x0 -> x1, starting transfers between devices: none -> 7.39 us  [shards(): lax.all_to_all(jnp.stack([project(col_features, col_proj)] * lax.axis_siz...]
    dot_general x9, matrix products: 3.75 us -> 9.43 us  [conv_taps(): jnp.einsum('co,cij->oij', weight[tap_row, tap_col], window, preferred_ele...]
    unnamed x41 -> x39, local copies, waits for them, and re-layouts: 10.3 us -> 11.6 us
  transfers between devices with their start and end apart: 18 -> 19, of which waited for: 5 -> 9; matrix products, arithmetic and copies ran while one was open for 10% -> 12% of each run, Pallas kernels for 0% -> 0%
where the time goes in v1:
time: 346 us; the launch traced here: 345 us
  waiting for transfers between devices  162 us (47%)
  blocking collectives  60.9 us (18%)
  starting transfers between devices  42.4 us (12%)
  matrix products  30.2 us (9%)
  between operations  24.6 us (7%)
  local copies, waits for them, and re-layouts  18.8 us (5%)
  other arithmetic  5.48 us (2%)
    psum x1, waiting for transfers between devices, shards(): lax.psum((grad_row_proj, grad_col_proj, jnp.stack([grad_row_pair, grad_co...  126 us
    psum x1, blocking collectives, shards(): lax.psum((grad_row_proj, grad_col_proj, jnp.stack([grad_row_pair, grad_co...  48 us
    ppermute x8, starting transfers between devices, padded_2(): before = lax.ppermute(last, axis, up)  24.6 us
    ppermute x8, waiting for transfers between devices, padded_2(): after = lax.ppermute(leading, axis, down)  17.1 us
    ppermute x8, waiting for transfers between devices, padded_2(): before = lax.ppermute(last, axis, up)  16.7 us
    unnamed x39, local copies, waits for them, and re-layouts  11.6 us
    ppermute x8, starting transfers between devices, padded_2(): after = lax.ppermute(leading, axis, down)  10.3 us
    dot_general x9, matrix products, conv_taps(): jnp.einsum('co,cij->oij', weight[tap_row, tap_col], window, preferred_ele...  9.43 us
  transfers between devices with their start and end apart: 19, of which 9 were waited for; matrix products, arithmetic and copies ran while one was open for 12% of the time, Pallas kernels for 0%

profile of v1, /device:TPU:0, one launch (start us, length us, event | category | flops | bytes accessed | tf_op | source)
XLA Modules:
  0.0 344.9 jit_solution(15591205327978352425)
XLA Ops:
  9.5 7.4 %all-to-all-start = ((bf16[16,2,512]{2,1,0:T(2,128)(2,1)}), bf16[16,2,512]{2,1,0:T(2,128)(2,1)S(1)}, u32[]{:S(2)}, u32[]{:S(2)}) async-start(bf16[16,2,512]{2,1,0:T(2,128)(2,1)} %reshape.186), calls=%async_computation | async-start | bytes 65536 | tf_op jit(solution)/shard_map/all_to_all | solution.py:137
  17.8 4.4 %all_gather.3 = bf16[16,64]{1,0:T(8,128)(2,1)S(1)} all-gather(bf16[8,64]{1,0:T(8,128)(2,1)S(1)} %convolution_convert_fusion.1), channel_id=1, replica_groups=mesh['row'=16,'col'=2] {'col'}, dimensions={0}, use_global_device_ids=true | all-gather | bytes 3072 | tf_op jit(solution)/shard_map/all_gather | solution.py:135
  22.2 1.4 collective-permute-start
  26.7 5.8 %collective-permute-start.8 = (bf16[64,8,256]{2,0,1:T(8,128)(2,1)}, bf16[64,8,256]{2,0,1:T(8,128)(2,1)}, u32[]{:S(2)}, u32[]{:S(2)}) collective-permute-start(bf16[64,8,256]{2,0,1:T(8,128)(2,1)} %copy.143), channel_id=1, source_target_pairs={{0,2},{2,4},{4,6},{6,8},{8,10},{10,12},{12,14},{14,16},{16,18},{18... | collective-permute-start | bytes 786440 | tf_op jit(solution)/shard_map/ppermute | solution.py:16
  46.3 1.3 fusion.85
  48.0 3.4 collective-permute-start.2
  52.8 4.1 %collective-permute-done.3 = bf16[8,64]{1,0:T(8,128)(2,1)S(1)} collective-permute-done((bf16[8,64]{1,0:T(8,128)(2,1)S(1)}, bf16[8,64]{1,0:T(8,128)(2,1)S(1)}, u32[]{:S(2)}, u32[]{:S(2)}) %collective-permute-start.3) | collective-permute-done | bytes 1056 | tf_op jit(solution)/shard_map/ppermute | solution.py:17
  57.9 1.3 multiply_convert_fusion
  60.4 2.2 collective-permute-start.4
  63.8 1.3 fusion.87
  67.5 2.0 collective-permute-start.10
  70.9 8.4 %collective-permute-done.10 = bf16[64,32,8]{2,0,1:T(8,128)(2,1)S(1)} collective-permute-done((bf16[64,32,8]{2,0,1:T(8,128)(2,1)S(1)}, bf16[64,32,8]{2,0,1:T(8,128)(2,1)S(1)}, u32[]{:S(2)}, u32[]{:S(2)}) %collective-permute-start.10) | collective-permute-done | bytes 32800 | tf_op jit(solution)/shard_map/ppermute | solution.py:16
  79.3 4.7 %collective-permute-done.11 = bf16[64,32,8]{2,0,1:T(8,128)(2,1)S(1)} collective-permute-done((bf16[64,32,8]{2,0,1:T(8,128)(2,1)S(1)}, bf16[64,32,8]{2,0,1:T(8,128)(2,1)S(1)}, u32[]{:S(2)}, u32[]{:S(2)}) %collective-permute-start.11) | collective-permute-done | bytes 32800 | tf_op jit(solution)/shard_map/ppermute | solution.py:17
  89.3 1.8 convolution_bitcast_fusion.7
  92.0 8.5 %psum.49 = f32[3,16,64]{1,0,2:T(4,128)S(1)} all-reduce(f32[3,16,64]{1,0,2:T(4,128)S(1)} %bitcast.309), channel_id=1, replica_groups=mesh['row'=16,'col'=2] {'col'}, use_global_device_ids=true, to_apply=%region_0.1 | all-reduce | flops 3072 | bytes 24576 | tf_op jit(solution)/shard_map/psum | solution.py:174
  101.1 2.2 collective-permute-start.12
  104.9 48.0 %psum.54 = f32[64]{0:T(128)} all-reduce(f32[64]{0:T(128)S(1)} %get-tuple-element.56), channel_id=1, replica_groups=mesh['row'=16,'col'=2] {'row','col'}, use_global_device_ids=true, to_apply=%region_6.7 | all-reduce | flops 64 | bytes 512 | tf_op jit(solution)/shard_map/psum | solution.py:244
  154.2 4.4 %collective-permute-start.6 = (bf16[64,32,8]{2,0,1:T(8,128)(2,1)S(1)}, bf16[64,32,8]{2,0,1:T(8,128)(2,1)S(1)}, u32[]{:S(2)}, u32[]{:S(2)}) collective-permute-start(bf16[64,32,8]{2,0,1:T(8,128)(2,1)S(1)} %get-tuple-element.22), channel_id=1, source_target_pairs={{0,1},{2,3},{4,5},{6,7},{8,9},{10,11},{12,13},{14,15},{16,17},{18,... | collective-permute-start | bytes 98312 | tf_op jit(solution)/shard_map/ppermute | solution.py:16
  160.7 8.1 %collective-permute-done.6 = bf16[64,32,8]{2,0,1:T(8,128)(2,1)S(1)} collective-permute-done((bf16[64,32,8]{2,0,1:T(8,128)(2,1)S(1)}, bf16[64,32,8]{2,0,1:T(8,128)(2,1)S(1)}, u32[]{:S(2)}, u32[]{:S(2)}) %collective-permute-start.6) | collective-permute-done | bytes 32800 | tf_op jit(solution)/shard_map/ppermute | solution.py:16
  168.7 4.1 %collective-permute-done.7 = bf16[64,32,8]{2,0,1:T(8,128)(2,1)S(1)} collective-permute-done((bf16[64,32,8]{2,0,1:T(8,128)(2,1)S(1)}, bf16[64,32,8]{2,0,1:T(8,128)(2,1)S(1)}, u32[]{:S(2)}, u32[]{:S(2)}) %collective-permute-start.7) | collective-permute-done | bytes 32800 | tf_op jit(solution)/shard_map/ppermute | solution.py:17
  178.8 1.4 fusion.49
  180.2 1.4 fusion.35
  181.5 1.4 fusion.46
  184.1 2.2 all-reduce.4.cloned.1.call-done
  186.4 1.7 constant_dynamic-slice_fusion.3
  190.4 3.3 collective-permute-start.14
  196.5 4.1 %collective-permute-done.15 = f32[3,8,64]{1,2,0:T(8,128)S(1)} collective-permute-done((f32[3,8,64]{1,2,0:T(8,128)S(1)}, f32[3,8,64]{1,2,0:T(8,128)S(1)}, u32[]{:S(2)}, u32[]{:S(2)}) %collective-permute-start.15) | collective-permute-done | bytes 6176 | tf_op jit(solution)/shard_map/ppermute | solution.py:17
  201.7 2.4 fusion.21
  205.9 126.3 %all-reduce.6.cloned.1.call-done = (f32[256,64]{0,1:T(8,128)}, f32[256,64]{0,1:T(8,128)}, f32[2,3,3,64,64]{3,4,1,2,0:T(8,128)}, f32[3,3,64,64]{3,2,1,0:T(8,128)}) async-done(((f32[256,64]{0,1:T(8,128)}, f32[256,64]{0,1:T(8,128)}, f32[2,3,3,64,64]{3,4,1,2,0:T(8,128)}, f32[3,3,64,64]{3,2,1,0:T(8,128)}), (f32[256,64]{0,1:T(8,128)}, f32[256,64]{0,1:T(8,128)}, f32[2,3,3,64,64]{3,4,1,2,0:T(8,128)}, ...) | async-done | bytes 573456 | tf_op jit(solution)/shard_map/psum | solution.py:244
  332.2 2.1 copy.59
  334.4 1.5 copy.156
  335.8 1.5 copy.157
  (133 shorter events, 46.2 us)
Async XLA Ops:
  7.2 0.8 copy-start
  7.2 39.1 %copy-start.1 = (bf16[64,16,256]{2,1,0:T(8,128)(2,1)S(1)}, bf16[64,16,256]{2,1,0:T(8,128)(2,1)}, u32[]{:S(2)}) copy-start(bf16[64,16,256]{2,1,0:T(8,128)(2,1)} %param.17) | copy-start | bytes 1572868
  7.2 27.4 %copy-start.11 = (s32[2]{0:T(128)S(1)}, s32[2]{0:T(128)}, u32[]{:S(2)}) copy-start(s32[2]{0:T(128)} %param.16) | copy-start | bytes 28
  7.2 39.1 %copy-start.4 = (bf16[3,3,64,64]{3,2,1,0:T(8,128)(2,1)S(1)}, bf16[3,3,64,64]{3,2,1,0:T(8,128)(2,1)}, u32[]{:S(2)}) copy-start(bf16[3,3,64,64]{3,2,1,0:T(8,128)(2,1)} %param.15) | copy-start | bytes 221188
  9.5 38.4 %all-to-all-start = ((bf16[16,2,512]{2,1,0:T(2,128)(2,1)}), bf16[16,2,512]{2,1,0:T(2,128)(2,1)S(1)}, u32[]{:S(2)}, u32[]{:S(2)}) async-start(bf16[16,2,512]{2,1,0:T(2,128)(2,1)} %reshape.186), calls=%async_computation | async-start | bytes 65536 | tf_op jit(solution)/shard_map/all_to_all | solution.py:137
  16.9 169.5 %all-reduce.4.cloned.1.call-start = ((), (), s32[]{:S(2)}) async-start(), calls=%async_computation.1 | async-start | bytes 524288 | tf_op jit(solution)/shard_map/psum | solution.py:175
  22.2 25.4 %collective-permute-start = (bf16[8,64]{1,0:T(8,128)(2,1)S(1)}, bf16[8,64]{1,0:T(8,128)(2,1)S(1)}, u32[]{:S(2)}, u32[]{:S(2)}) collective-permute-start(bf16[8,64]{1,0:T(8,128)(2,1)S(1)} %get-tuple-element.51), channel_id=1, source_target_pairs={{0,2},{2,4},{4,6},{6,8},{8,10},{10,12},{12,14},{14,16},{16,18},{18... | collective-permute-start | bytes 3080 | tf_op jit(solution)/shard_map/ppermute | solution.py:16
  23.6 24.1 %collective-permute-start.1 = (bf16[8,64]{1,0:T(8,128)(2,1)S(1)}, bf16[8,64]{1,0:T(8,128)(2,1)S(1)}, u32[]{:S(2)}, u32[]{:S(2)}) collective-permute-start(bf16[8,64]{1,0:T(8,128)(2,1)S(1)} %get-tuple-element.50), channel_id=1, source_target_pairs={{2,0},{4,2},{6,4},{8,6},{10,8},{12,10},{14,12},{16,14},{18,16},{20... | collective-permute-start | bytes 3080 | tf_op jit(solution)/shard_map/ppermute | solution.py:17
  25.9 21.8 %copy-start.7 = (bf16[2,3,3,64,64]{4,3,2,1,0:T(8,128)(2,1)S(1)}, bf16[2,3,3,64,64]{4,3,2,1,0:T(8,128)(2,1)}, u32[]{:S(2)}) copy-start(bf16[2,3,3,64,64]{4,3,2,1,0:T(8,128)(2,1)} %param.13) | copy-start | bytes 442372
  26.7 38.4 %collective-permute-start.8 = (bf16[64,8,256]{2,0,1:T(8,128)(2,1)}, bf16[64,8,256]{2,0,1:T(8,128)(2,1)}, u32[]{:S(2)}, u32[]{:S(2)}) collective-permute-start(bf16[64,8,256]{2,0,1:T(8,128)(2,1)} %copy.143), channel_id=1, source_target_pairs={{0,2},{2,4},{4,6},{6,8},{8,10},{10,12},{12,14},{14,16},{16,18},{18... | collective-permute-start | bytes 786440 | tf_op jit(solution)/shard_map/ppermute | solution.py:16
  33.3 33.0 %collective-permute-start.9 = (bf16[64,8,256]{2,0,1:T(8,128)(2,1)}, bf16[64,8,256]{2,0,1:T(8,128)(2,1)}, u32[]{:S(2)}, u32[]{:S(2)}) collective-permute-start(bf16[64,8,256]{2,0,1:T(8,128)(2,1)} %copy.144), channel_id=1, source_target_pairs={{2,0},{4,2},{6,4},{8,6},{10,8},{12,10},{14,12},{16,14},{18,16},{20... | collective-permute-start | bytes 786440 | tf_op jit(solution)/shard_map/ppermute | solution.py:17
  47.6 10.3 %copy-start.12 = (f32[64]{0:T(128)S(1)}, f32[64]{0:T(128)}, u32[]{:S(2)}) copy-start(f32[64]{0:T(128)} %param.14) | copy-start | bytes 772
  48.0 4.8 %collective-permute-start.2 = (bf16[8,64]{1,0:T(8,128)(2,1)S(1)}, bf16[8,64]{1,0:T(8,128)(2,1)S(1)}, u32[]{:S(2)}, u32[]{:S(2)}) collective-permute-start(bf16[8,64]{1,0:T(8,128)(2,1)S(1)} %get-tuple-element.38), channel_id=1, source_target_pairs={{0,1},{2,3},{4,5},{6,7},{8,9},{10,11},{12,13},{14,15},{16,17},{18,... | collective-permute-start | bytes 3080 | tf_op jit(solution)/shard_map/ppermute | solution.py:16
  51.5 5.5 %collective-permute-start.3 = (bf16[8,64]{1,0:T(8,128)(2,1)S(1)}, bf16[8,64]{1,0:T(8,128)(2,1)S(1)}, u32[]{:S(2)}, u32[]{:S(2)}) collective-permute-start(bf16[8,64]{1,0:T(8,128)(2,1)S(1)} %get-tuple-element.39), channel_id=1, source_target_pairs={{1,0},{3,2},{5,4},{7,6},{9,8},{11,10},{13,12},{15,14},{17,16},{19,... | collective-permute-start | bytes 3080 | tf_op jit(solution)/shard_map/ppermute | solution.py:17
  60.4 93.4 %collective-permute-start.4 = (bf16[64,8,256]{2,0,1:T(8,128)(2,1)}, bf16[64,8,256]{2,0,1:T(8,128)(2,1)S(1)}, u32[]{:S(2)}, u32[]{:S(2)}) collective-permute-start(bf16[64,8,256]{2,0,1:T(8,128)(2,1)} %get-tuple-element.26), channel_id=1, source_target_pairs={{0,2},{2,4},{4,6},{6,8},{8,10},{10,12},{12,14},{14,16},{16,18},{18... | collective-permute-start | bytes 786440 | tf_op jit(solution)/shard_map/ppermute | solution.py:16
  62.5 91.3 %collective-permute-start.5 = (bf16[64,8,256]{2,0,1:T(8,128)(2,1)S(1)}, bf16[64,8,256]{2,0,1:T(8,128)(2,1)S(1)}, u32[]{:S(2)}, u32[]{:S(2)}) collective-permute-start(bf16[64,8,256]{2,0,1:T(8,128)(2,1)S(1)} %get-tuple-element.27), channel_id=1, source_target_pairs={{2,0},{4,2},{6,4},{8,6},{10,8},{12,10},{14,12},{16,14},{18,16},{20... | collective-permute-start | bytes 786440 | tf_op jit(solution)/shard_map/ppermute | solution.py:17
  67.5 11.7 %collective-permute-start.10 = (bf16[64,32,8]{2,0,1:T(8,128)(2,1)S(1)}, bf16[64,32,8]{2,0,1:T(8,128)(2,1)S(1)}, u32[]{:S(2)}, u32[]{:S(2)}) collective-permute-start(bf16[64,32,8]{2,0,1:T(8,128)(2,1)S(1)} %get-tuple-element.20), channel_id=1, source_target_pairs={{0,1},{2,3},{4,5},{6,7},{8,9},{10,11},{12,13},{14,15},{16,17},{18,... | collective-permute-start | bytes 98312 | tf_op jit(solution)/shard_map/ppermute | solution.py:16
  69.5 14.5 %collective-permute-start.11 = (bf16[64,32,8]{2,0,1:T(8,128)(2,1)S(1)}, bf16[64,32,8]{2,0,1:T(8,128)(2,1)S(1)}, u32[]{:S(2)}, u32[]{:S(2)}) collective-permute-start(bf16[64,32,8]{2,0,1:T(8,128)(2,1)S(1)} %get-tuple-element.21), channel_id=1, source_target_pairs={{1,0},{3,2},{5,4},{7,6},{9,8},{11,10},{13,12},{15,14},{17,16},{19,... | collective-permute-start | bytes 98312 | tf_op jit(solution)/shard_map/ppermute | solution.py:17
  86.6 1.2 copy-start.3
  91.1 61.9 %copy-start.10 = (bf16[8,256]{1,0:T(8,128)(2,1)S(1)}, bf16[8,256]{1,0:T(8,128)(2,1)}, u32[]{:S(2)}) copy-start(bf16[8,256]{1,0:T(8,128)(2,1)} %param.9) | copy-start | bytes 12292
  91.8 240.4 %all-reduce.6.cloned.1.call-start = ((), (), s32[]{:S(2)}) async-start(), calls=%async_computation.2 | async-start | bytes 2031616 | tf_op jit(solution)/shard_map/psum | solution.py:244
  101.1 51.8 %collective-permute-start.12 = (f32[3,8,64]{2,1,0:T(8,128)S(1)}, f32[3,8,64]{2,1,0:T(8,128)S(1)}, u32[]{:S(2)}, u32[]{:S(2)}) collective-permute-start(f32[3,8,64]{2,1,0:T(8,128)S(1)} %get-tuple-element.43), channel_id=1, source_target_pairs={{0,2},{2,4},{4,6},{6,8},{8,10},{10,12},{12,14},{14,16},{16,18},{18... | collective-permute-start | bytes 18440 | tf_op jit(solution)/shard_map/ppermute | solution.py:16
  103.3 49.6 %collective-permute-start.13 = (f32[3,8,64]{2,1,0:T(8,128)S(1)}, f32[3,8,64]{2,1,0:T(8,128)S(1)}, u32[]{:S(2)}, u32[]{:S(2)}) collective-permute-start(f32[3,8,64]{2,1,0:T(8,128)S(1)} %get-tuple-element.44), channel_id=1, source_target_pairs={{2,0},{4,2},{6,4},{8,6},{10,8},{12,10},{14,12},{16,14},{18,16},{20... | collective-permute-start | bytes 18440 | tf_op jit(solution)/shard_map/ppermute | solution.py:17
  153.9 6.0 %copy-start.8 = (bf16[256,64]{0,1:T(8,128)(2,1)S(1)}, bf16[256,64]{0,1:T(8,128)(2,1)}, u32[]{:S(2)}) copy-start(bf16[256,64]{0,1:T(8,128)(2,1)} %param.11) | copy-start | bytes 98308
  154.2 14.5 %collective-permute-start.6 = (bf16[64,32,8]{2,0,1:T(8,128)(2,1)S(1)}, bf16[64,32,8]{2,0,1:T(8,128)(2,1)S(1)}, u32[]{:S(2)}, u32[]{:S(2)}) collective-permute-start(bf16[64,32,8]{2,0,1:T(8,128)(2,1)S(1)} %get-tuple-element.22), channel_id=1, source_target_pairs={{0,1},{2,3},{4,5},{6,7},{8,9},{10,11},{12,13},{14,15},{16,17},{18,... | collective-permute-start | bytes 98312 | tf_op jit(solution)/shard_map/ppermute | solution.py:16
  158.6 14.2 %collective-permute-start.7 = (bf16[64,32,8]{2,0,1:T(8,128)(2,1)S(1)}, bf16[64,32,8]{2,0,1:T(8,128)(2,1)S(1)}, u32[]{:S(2)}, u32[]{:S(2)}) collective-permute-start(bf16[64,32,8]{2,0,1:T(8,128)(2,1)S(1)} %get-tuple-element.23), channel_id=1, source_target_pairs={{1,0},{3,2},{5,4},{7,6},{9,8},{11,10},{13,12},{15,14},{17,16},{19,... | collective-permute-start | bytes 98312 | tf_op jit(solution)/shard_map/ppermute | solution.py:17
  176.2 1.4 copy-start.5
  180.1 2.8 copy-start.2
  190.3 10.6 %copy-start.9 = (bf16[16,256]{1,0:T(8,128)(2,1)S(1)}, bf16[16,256]{1,0:T(8,128)(2,1)}, u32[]{:S(2)}) copy-start(bf16[16,256]{1,0:T(8,128)(2,1)} %param.10) | copy-start | bytes 24580
  190.4 6.0 %collective-permute-start.14 = (f32[3,8,64]{1,2,0:T(8,128)S(1)}, f32[3,8,64]{1,2,0:T(8,128)S(1)}, u32[]{:S(2)}, u32[]{:S(2)}) collective-permute-start(f32[3,8,64]{1,2,0:T(8,128)S(1)} %get-tuple-element.31), channel_id=1, source_target_pairs={{0,1},{2,3},{4,5},{6,7},{8,9},{10,11},{12,13},{14,15},{16,17},{18,... | collective-permute-start | bytes 18440 | tf_op jit(solution)/shard_map/ppermute | solution.py:16
  193.8 6.8 %collective-permute-start.15 = (f32[3,8,64]{1,2,0:T(8,128)S(1)}, f32[3,8,64]{1,2,0:T(8,128)S(1)}, u32[]{:S(2)}, u32[]{:S(2)}) collective-permute-start(f32[3,8,64]{1,2,0:T(8,128)S(1)} %get-tuple-element.32), channel_id=1, source_target_pairs={{1,0},{3,2},{5,4},{7,6},{9,8},{11,10},{13,12},{15,14},{17,16},{19,... | collective-permute-start | bytes 18440 | tf_op jit(solution)/shard_map/ppermute | solution.py:17
  332.2 5.1 %copy-start.6 = (f32[3,3,64,64]{3,2,1,0:T(8,128)S(1)}, f32[3,3,64,64]{3,2,1,0:T(8,128)}, u32[]{:S(2)}) copy-start(f32[3,3,64,64]{3,2,1,0:T(8,128)} %get-tuple-element.69) | copy-start | bytes 442372
Sparse Core Ops, SparseCore 0:
  92.0 94.3 all-reduce.3
  201.8 130.3 all-reduce.5
